TPU v7x, 32 devices: a whole 2x2x4 slice. The times are simulated.
32 devices in a mesh: groups: 2 (over x), wide: 16 (over z, y, core).
Axes of the slice: x: 2, y: 2, z: 4, core: 2. Of those that a mesh axis runs over, the one named last changes fastest.
Arguments:
- prefix_hidden: bfloat16 [32, 256, 8192], P(('groups', 'wide')), parts along dimension 0, may hold values from -6 to 6
- prefix_lengths: int32 [32], P(('groups', 'wide')), parts along dimension 0, may hold values from 64 to 256
- action_noise: float32 [32, 50, 32], P(('groups', 'wide')), parts along dimension 0, may hold values from -4 to 4
- prefix_gain: float32 [8192], replicated, may hold values from 0.1 to 1.9
- key_weight: bfloat16 [8192, 512], P('wide'), may hold values from -0.0625 to 0.0625
- value_weight: bfloat16 [8192, 512], P('wide'), may hold values from -0.0625 to 0.0625
- input_weight: float32 [32, 1024], replicated, may hold values from -1 to 1
- expert_gain: float32 [1024], replicated, may hold values from 0.1 to 1.9
- expert_query: bfloat16 [1024, 1024], P('wide'), may hold values from -0.1875 to 0.1875
- expert_key: bfloat16 [1024, 512], P('wide'), may hold values from -5.3125 to 5.3125
- expert_value: bfloat16 [1024, 512], P('wide'), may hold values from -0.1875 to 0.1875
- expert_output: bfloat16 [1024, 1024], P('wide'), may hold values from -0.1875 to 0.1875
- final_gain: float32 [1024], replicated, may hold values from 0.1 to 1.9
- output_weight: bfloat16 [1024, 32], replicated, may hold values from -0.1875 to 0.1875
Outputs:
- actions: float32 [32, 50, 32], P(('groups', 'wide')), parts along dimension 0
There are 2 independent parts, one for each index of `groups`. A program takes and returns all parts, laid end to end along the dimension named above; an argument that names none is the same for every part. Nothing has to cross between parts.
Inputs may be any that keep to these rules, and one draw needn't show every extreme that they name: `prefix_lengths`: positions at or after a sample's length are padding and take no part.
All inputs are finite; a program needn't handle non-finite values.
Results may differ from a plain program's by a relative error of at most 0.0075.
Values may be sent and summed in bfloat16 or wider, within the bound.
A program may use at most 128 MiB of HBM per device.

v0:
```python
import jax
import jax.numpy as jnp
from jax import lax
from jax.sharding import PartitionSpec as P

HEAD = 128
STEPS = 4


rope_base = 1000000.0
norm_eps = 1e-06


def normalize(values, norm_gain):
    mean_square = jnp.mean(values * values, axis=-1, keepdims=True)
    return values * lax.rsqrt(mean_square + norm_eps) * norm_gain


def rotate(values, positions):
    half_width = values.shape[-1] // 2
    inv_freqs = rope_base ** (-jnp.arange(half_width, dtype=jnp.float32) * 2.0 / values.shape[-1])
    angles = positions[:, None] * inv_freqs[None, :]
    cosine = jnp.cos(angles)[:, None, :]
    sine_part = jnp.sin(angles)[:, None, :]
    first_half = values[..., :half_width]
    second = values[..., half_width:]
    return jnp.concatenate(
        [first_half * cosine - second * sine_part, second * cosine + first_half * sine_part], -1
    )


def time_embedding(time_value, embed_width):
    half_width = embed_width // 2
    fraction = jnp.arange(half_width, dtype=jnp.float32) / (half_width - 1)
    period = 0.004 * (4.0 / 0.004) ** fraction
    angles = time_value * (2.0 * jnp.pi) / period
    return jnp.concatenate([jnp.sin(angles), jnp.cos(angles)])


def attend(queries, key_cache, value_cache, action_keys, action_values, is_valid):
    span_rows = queries.shape[0]
    groups = key_cache.shape[1] // HEAD
    group_ratio = queries.shape[1] // key_cache.shape[1]
    query_heads = queries.reshape(span_rows, groups, group_ratio, HEAD)
    prefix_keys = key_cache.reshape(-1, groups, HEAD)
    prefix_values = value_cache.reshape(-1, groups, HEAD)
    own_keys = action_keys.reshape(span_rows, groups, HEAD)
    own_values = action_values.reshape(span_rows, groups, HEAD)
    prefix_scores = jnp.einsum(
        "cgrh,pgh->grcp", query_heads, prefix_keys, preferred_element_type=jnp.float32
    )
    prefix_scores = jnp.where(is_valid[None, None, None, :], prefix_scores, -1e30)
    own_scores = jnp.einsum(
        "cgrh,ngh->grcn", query_heads, own_keys, preferred_element_type=jnp.float32
    )
    row_max = jnp.maximum(jnp.max(prefix_scores, -1), jnp.max(own_scores, -1))[..., None]
    prefix_exp = jnp.exp(prefix_scores - row_max)
    own_exp = jnp.exp(own_scores - row_max)
    prob_total = jnp.sum(prefix_exp, -1, keepdims=True) + jnp.sum(own_exp, -1, keepdims=True)
    prefix_prob = (prefix_exp / prob_total).astype(jnp.bfloat16)
    own_prob = (own_exp / prob_total).astype(jnp.bfloat16)
    attn_mixed = jnp.einsum(
        "grcp,pgh->cgrh", prefix_prob, prefix_values, preferred_element_type=jnp.float32
    )
    attn_mixed = attn_mixed + jnp.einsum(
        "grcn,ngh->cgrh", own_prob, own_values, preferred_element_type=jnp.float32
    )
    return attn_mixed.reshape(span_rows, -1).astype(jnp.bfloat16)


def expert_steps(
    noise_rows,
    length,
    input_weight,
    expert_gain,
    query_w,
    key_w,
    value_w,
    output_w,
    final_gain,
    output_weight,
    key_cache,
    value_cache,
):
    span_rows = noise_rows.shape[0]
    is_valid = jnp.arange(key_cache.shape[0], dtype=jnp.int32) < length
    positions = length.astype(jnp.float32) + jnp.arange(span_rows, dtype=jnp.float32)
    action_state = noise_rows
    for step_idx in range(STEPS):
        time_value = 1.0 - step_idx / STEPS
        hidden = jnp.dot(
            action_state,
            input_weight,
            precision=lax.Precision.HIGHEST,
            preferred_element_type=jnp.float32,
        )
        hidden = hidden + time_embedding(time_value, input_weight.shape[1])[None, :]
        normed = normalize(hidden, expert_gain).astype(jnp.bfloat16)
        raw_queries = jnp.dot(normed, query_w, preferred_element_type=jnp.float32)
        queries = rotate(raw_queries.reshape(span_rows, -1, HEAD), positions).reshape(span_rows, -1)
        queries = (queries * HEAD ** (-0.5)).astype(jnp.bfloat16)
        raw_keys = jnp.dot(normed, key_w, preferred_element_type=jnp.float32)
        action_keys = (
            rotate(raw_keys.reshape(span_rows, -1, HEAD), positions)
            .reshape(span_rows, -1)
            .astype(jnp.bfloat16)
        )
        action_values = jnp.dot(normed, value_w, preferred_element_type=jnp.float32).astype(
            jnp.bfloat16
        )
        attn_mixed = attend(queries, key_cache, value_cache, action_keys, action_values, is_valid)
        hidden = hidden + jnp.dot(attn_mixed, output_w, preferred_element_type=jnp.float32)
        final_normed = normalize(hidden, final_gain).astype(jnp.bfloat16)
        velocity = jnp.dot(final_normed, output_weight, preferred_element_type=jnp.float32)
        action_state = action_state - velocity / STEPS
    return action_state


def shards(
    prefix_hidden,
    prefix_lengths,
    action_noise,
    prefix_gain,
    key_weight,
    value_weight,
    input_weight,
    expert_gain,
    expert_query,
    expert_key,
    expert_value,
    expert_output,
    final_gain,
    output_weight,
):
    gathered = (
        lax.all_gather(expert_query, "wide", axis=0, tiled=True),
        lax.all_gather(expert_key, "wide", axis=0, tiled=True),
        lax.all_gather(expert_value, "wide", axis=0, tiled=True),
        lax.all_gather(expert_output, "wide", axis=0, tiled=True),
    )
    hidden = prefix_hidden[0]
    row_count = hidden.shape[0]
    normed = normalize(hidden.astype(jnp.float32), prefix_gain).astype(jnp.bfloat16)
    stacked = jnp.stack([key_weight, value_weight], 0)
    projected = jnp.einsum(
        "pd,kdc->pkc",
        normed,
        lax.all_gather(stacked, "wide", axis=1, tiled=True),
        preferred_element_type=jnp.float32,
    )
    positions = jnp.arange(row_count, dtype=jnp.float32)
    key_cache = (
        rotate(projected[:, 0].reshape(row_count, -1, HEAD), positions)
        .reshape(row_count, -1)
        .astype(jnp.bfloat16)
    )
    value_cache = projected[:, 1].astype(jnp.bfloat16)
    query_w, key_w, value_w, output_w = gathered
    action_state = expert_steps(
        action_noise[0],
        prefix_lengths[0],
        input_weight,
        expert_gain,
        query_w,
        key_w,
        value_w,
        output_w,
        final_gain,
        output_weight,
        key_cache,
        value_cache,
    )
    return action_state[None]


def solution(mesh):
    placed = (
        P(("groups", "wide"), None, None),
        P(("groups", "wide")),
        P(("groups", "wide"), None, None),
        P(),
        P("wide", None),
        P("wide", None),
        P(),
        P(),
        P("wide", None),
        P("wide", None),
        P("wide", None),
        P("wide", None),
        P(),
        P(),
    )
    return jax.shard_map(
        shards,
        mesh=mesh,
        in_specs=placed,
        out_specs=P(("groups", "wide"), None, None),
        check_vma=False,
    )
```

profile of v0, /device:TPU:0, one launch (start us, length us, event | category | flops | bytes accessed | tf_op | source)
XLA Modules:
  0.0 368.0 jit_solution(7898720133912089493)
XLA Ops:
  8.8 2.3 pad_maximum_fusion
  12.0 3.1 fusion
  19.0 31.2 %all-gather.10.cloned.1.call-done = bf16[1024,512]{1,0:T(8,128)(2,1)} async-done(((bf16[64,512]{1,0:T(8,128)(2,1)}), bf16[1024,512]{1,0:T(8,128)(2,1)}) %all-gather.10.cloned.1.call-update) | async-done | bytes 1048592 | tf_op jit(solution)/shard_map/all_gather | solution.py:137
  50.2 1.5 fusion.107
  51.9 37.4 %all-gather.12.cloned.1.call-done = bf16[1024,512]{1,0:T(8,128)(2,1)} async-done(((bf16[64,512]{1,0:T(8,128)(2,1)}), bf16[1024,512]{1,0:T(8,128)(2,1)}) %all-gather.12.cloned.1.call-update) | async-done | bytes 1048592 | tf_op jit(solution)/shard_map/all_gather | solution.py:138
  89.2 1.5 convolution_convert_fusion.3
  91.4 40.4 %all-gather.8.cloned.1.call-done = bf16[1024,1024]{1,0:T(8,128)(2,1)} async-done(((bf16[64,1024]{1,0:T(8,128)(2,1)}), bf16[1024,1024]{1,0:T(8,128)(2,1)}) %all-gather.8.cloned.1.call-update) | async-done | bytes 2097168 | tf_op jit(solution)/shard_map/all_gather | solution.py:136
  131.9 2.1 fusion.106
  134.6 124.5 %all-gather.6.cloned.1.call-done = bf16[2,8192,512]{2,1,0:T(8,128)(2,1)} async-done(((bf16[2,512,512]{2,1,0:T(8,128)(2,1)}), bf16[2,8192,512]{2,1,0:T(8,128)(2,1)}) %all-gather.6.cloned.1.call-update) | async-done | bytes 16777232 | tf_op jit(solution)/shard_map/all_gather | solution.py:148
  259.1 9.5 %fusion.4 = f32[256,2,512]{2,0,1:T(8,128)S(1)} fusion(bf16[2,8192,512]{2,1,0:T(8,128)(2,1)} %all-gather.6.cloned.1.call-done, bf16[1,256,8192]{2,1,0:T(8,128)(2,1)} %param.14, f32[8192]{0:T(1024)S(1)} %copy-done.58, f32[256]{0:T(256)S(1)} %add_rsqrt_fusion), kind=kOutput, calls=%fused_computation.6 | convolution fusion | flops 4303355904 | bytes 22053888 | tf_op jit(solution)/shard_map/pd,kdc->pkc/dot_general | solution.py:145
  271.2 29.5 %all-gather.14.cloned.1.call-done = bf16[1024,1024]{1,0:T(8,128)(2,1)} async-done(((bf16[64,1024]{1,0:T(8,128)(2,1)}), bf16[1024,1024]{1,0:T(8,128)(2,1)}) %all-gather.14.cloned.1.call-update) | async-done | bytes 2097168 | tf_op jit(solution)/shard_map/all_gather | solution.py:139
  300.8 2.2 multiply_reduce_fusion.6
  306.0 1.7 fusion.100
  307.7 0.9 fusion.109
  308.6 1.6 reshape.311
  310.2 1.1 fusion.96
  311.3 0.8 subtract_convert_fusion.3
  312.1 1.2 fusion.101
  314.1 1.3 fusion.27
  315.5 2.1 fusion.31
  317.6 0.9 convolution_convert_fusion.2
  318.5 1.5 reshape.312
  320.0 1.3 fusion.19
  321.3 0.7 copy.50
  322.0 1.6 convert_element_type.174
  323.6 2.2 multiply_reduce_fusion.4
  329.0 1.1 fusion.102
  330.1 0.9 fusion.111
  331.1 1.6 reshape.314
  332.6 1.1 fusion.95
  333.7 0.8 subtract_convert_fusion.2
  334.5 1.2 fusion.103
  335.7 1.4 fusion.28
  337.2 2.1 fusion.32
  339.3 0.9 convolution_convert_fusion.1
  340.2 1.5 reshape.315
  341.7 1.3 fusion.18
  343.0 0.7 copy.57
  343.7 1.6 convert_element_type.184
  345.3 2.2 multiply_reduce_fusion.2
  347.6 1.0 fusion.23
  348.6 1.2 multiply_reduce_fusion.1
  350.5 0.8 multiply_convert_fusion.1
  354.5 2.3 fusion.33
  356.7 0.9 convolution_convert_fusion
  357.7 0.9 reshape.318
  358.5 1.3 fusion.17
  360.6 0.8 fusion.22
  (221 shorter events, 21.2 us)
Async XLA Ops:
  6.5 9.1 %copy-start = (f32[32,1024]{1,0:T(8,128)S(1)}, f32[32,1024]{1,0:T(8,128)}, u32[]{:S(2)}) copy-start(f32[32,1024]{1,0:T(8,128)} %param.20) | copy-start | bytes 393220
  6.5 43.7 %all-gather.10.cloned.1.call-start = ((), (), s32[]{:S(2)}) async-start(), calls=%async_computation.2 | async-start | bytes 1114112 | tf_op jit(solution)/shard_map/all_gather | solution.py:137
  7.3 82.0 %all-gather.12.cloned.1.call-start = ((), (), s32[]{:S(2)}) async-start(), calls=%async_computation.3 | async-start | bytes 1114112 | tf_op jit(solution)/shard_map/all_gather | solution.py:138
  8.0 123.8 %all-gather.8.cloned.1.call-start = ((), (), s32[]{:S(2)}) async-start(), calls=%async_computation.1 | async-start | bytes 2228224 | tf_op jit(solution)/shard_map/all_gather | solution.py:136
  8.7 250.4 %all-gather.6.cloned.1.call-start = ((), (), s32[]{:S(2)}) async-start(), calls=%async_computation | async-start | bytes 17825792 | tf_op jit(solution)/shard_map/all_gather | solution.py:148
  11.1 289.7 %all-gather.14.cloned.1.call-start = ((), (), s32[]{:S(2)}) async-start(), calls=%async_computation.4 | async-start | bytes 2228224 | tf_op jit(solution)/shard_map/all_gather | solution.py:139
  11.9 3.7 %copy-start.44 = (f32[1,50,32]{1,2,0:T(8,128)S(1)}, f32[1,50,32]{1,2,0:T(8,128)}, u32[]{:S(2)}) copy-start(f32[1,50,32]{1,2,0:T(8,128)} %param.16) | copy-start | bytes 19204
  12.0 6.9 %copy-start.41 = (f32[1024]{0:T(1024)S(1)}, f32[1024]{0:T(1024)}, u32[]{:S(2)}) copy-start(f32[1024]{0:T(1024)} %param.21) | copy-start | bytes 12292
  16.1 117.8 %copy-start.17 = (f32[50,1024]{1,0:T(8,128)}, f32[50,1024]{1,0:T(8,128)S(1)}, u32[]{:S(2)}) copy-start(f32[50,1024]{1,0:T(8,128)S(1)} %get-tuple-element.38) | copy-start | bytes 614404
  17.0 117.0 %copy-start.7 = (f32[50,64]{1,0:T(8,128)}, f32[50,64]{1,0:T(8,128)S(1)}, u32[]{:S(2)}) copy-start(f32[50,64]{1,0:T(8,128)S(1)} %get-tuple-element.33) | copy-start | bytes 38404
  17.0 117.0 %copy-start.12 = (f32[50,64]{1,0:T(8,128)}, f32[50,64]{1,0:T(8,128)S(1)}, u32[]{:S(2)}) copy-start(f32[50,64]{1,0:T(8,128)S(1)} %get-tuple-element.34) | copy-start | bytes 38404
  17.0 252.6 %copy-start.53 = (pred[256]{0:T(512)(128)(4,1)}, pred[256]{0:T(512)(128)(4,1)S(1)}, u32[]{:S(2)}) copy-start(pred[256]{0:T(512)(128)(4,1)S(1)} %iota_compare_fusion) | copy-start | bytes 772
  91.4 167.7 %copy-start.58 = (f32[8192]{0:T(1024)S(1)}, f32[8192]{0:T(1024)}, u32[]{:S(2)}) copy-start(f32[8192]{0:T(1024)} %param.17) | copy-start | bytes 98308
  270.1 30.6 %copy-start.18 = (f32[50,1024]{1,0:T(8,128)S(1)}, f32[50,1024]{1,0:T(8,128)}, u32[]{:S(2)}) copy-start(f32[50,1024]{1,0:T(8,128)} %copy-done.17) | copy-start | bytes 614404
  270.8 32.2 %copy-start.30 = (bf16[1024,32]{0,1:T(8,128)(2,1)S(1)}, bf16[1024,32]{0,1:T(8,128)(2,1)}, u32[]{:S(2)}) copy-start(bf16[1024,32]{0,1:T(8,128)(2,1)} %param.27) | copy-start | bytes 196612
  270.8 32.2 %copy-start.45 = (f32[1,50,32]{1,2,0:T(8,128)S(1)}, f32[1,50,32]{1,2,0:T(8,128)}, u32[]{:S(2)}) copy-start(f32[1,50,32]{1,2,0:T(8,128)} %param.16) | copy-start | bytes 19204
  270.8 32.2 %copy-start.46 = (f32[1024]{0:T(1024)S(1)}, f32[1024]{0:T(1024)}, u32[]{:S(2)}) copy-start(f32[1024]{0:T(1024)} %param.26) | copy-start | bytes 12292
  270.8 32.4 %copy-start.52 = (f32[1024]{0:T(1024)S(1)}, f32[1024]{0:T(1024)}, u32[]{:S(2)}) copy-start(f32[1024]{0:T(1024)} %pad_maximum_fusion.2) | copy-start | bytes 12292
  271.1 32.7 %copy-start.42 = (f32[1024]{0:T(1024)S(1)}, f32[1024]{0:T(1024)}, u32[]{:S(2)}) copy-start(f32[1024]{0:T(1024)} %param.21) | copy-start | bytes 12292
  271.1 33.4 %copy-start.1 = (bf16[1024,1024]{1,0:T(8,128)(2,1)S(1)}, bf16[1024,1024]{1,0:T(8,128)(2,1)}, u32[]{:S(2)}) copy-start(bf16[1024,1024]{1,0:T(8,128)(2,1)} %all-gather.8.cloned.1.call-done) | copy-start | bytes 6291460
  303.2 1.8 copy-start.8
  303.2 1.8 copy-start.13
  304.4 3.2 copy-start.25
  304.9 2.7 copy-start.4
  310.2 7.4 %copy-start.3 = (bf16[1024,512]{1,0:T(8,128)(2,1)S(1)}, bf16[1024,512]{1,0:T(8,128)(2,1)}, u32[]{:S(2)}) copy-start(bf16[1024,512]{1,0:T(8,128)(2,1)} %all-gather.12.cloned.1.call-done) | copy-start | bytes 3145732
  310.2 7.4 %copy-start.26 = (bf16[50,1024]{1,0:T(8,128)(2,1)S(1)}, bf16[50,1024]{1,0:T(8,128)(2,1)}, u32[]{:S(2)}) copy-start(bf16[50,1024]{1,0:T(8,128)(2,1)} %copy-done.25) | copy-start | bytes 307204
  313.3 2.0 copy-start.37
  315.4 2.1 copy-start.57
  323.6 2.3 copy-start.31
  323.6 2.3 copy-start.47
  323.6 2.5 copy-start.51
  323.6 3.7 %copy-start.43 = (f32[1024]{0:T(1024)S(1)}, f32[1024]{0:T(1024)}, u32[]{:S(2)}) copy-start(f32[1024]{0:T(1024)} %param.21) | copy-start | bytes 12292
  326.1 1.9 copy-start.40
  326.2 1.9 copy-start.9
  326.2 1.9 copy-start.14
  327.4 2.7 copy-start.27
  327.9 2.2 copy-start.5
  332.6 6.7 %copy-start.28 = (bf16[50,1024]{1,0:T(8,128)(2,1)S(1)}, bf16[50,1024]{1,0:T(8,128)(2,1)}, u32[]{:S(2)}) copy-start(bf16[50,1024]{1,0:T(8,128)(2,1)} %copy-done.27) | copy-start | bytes 307204
  345.3 2.2 copy-start.32
  348.5 3.3 copy-start.10
  348.5 3.3 copy-start.15
  351.8 1.6 copy-start.11
  351.9 1.6 copy-start.16
  353.3 3.4 copy-start.24
  354.5 5.5 %copy-start.2 = (bf16[1024,1024]{1,0:T(8,128)(2,1)S(1)}, bf16[1024,1024]{1,0:T(8,128)(2,1)}, u32[]{:S(2)}) copy-start(bf16[1024,1024]{1,0:T(8,128)(2,1)} %all-gather.14.cloned.1.call-done) | copy-start | bytes 6291460
  354.5 5.5 %copy-start.20 = (f32[50,1024]{1,0:T(8,128)S(1)}, f32[50,1024]{1,0:T(8,128)}, u32[]{:S(2)}) copy-start(f32[50,1024]{1,0:T(8,128)} %copy-done.19) | copy-start | bytes 614404
  357.6 2.9 copy-start.33
  357.6 2.9 copy-start.48
  (16 other events, 17.1 us)
Sparse Core Ops, SparseCore 0:
  9.5 40.6 all-gather.9
  52.4 36.8 all-gather.11
  91.4 40.4 all-gather.7
  133.9 125.1 all-gather.5
  261.1 39.6 all-gather.13
where the time goes:
time: 369 us; the launch traced here: 368 us
  waiting for transfers between devices  266 us (72%)
  matrix products  50.5 us (14%)
  local copies, waits for them, and re-layouts  20.1 us (5%)
  other arithmetic  16.4 us (4%)
  between operations  15.1 us (4%)
    all_gather x1, waiting for transfers between devices, shards(): lax.all_gather(stacked, 'wide', axis=1, tiled=True)  124 us
    all_gather x1, waiting for transfers between devices, shards(): lax.all_gather(expert_query, 'wide', axis=0, tiled=True)  40.4 us
    all_gather x1, waiting for transfers between devices, shards(): lax.all_gather(expert_value, 'wide', axis=0, tiled=True)  37.4 us
    all_gather x1, waiting for transfers between devices, shards(): lax.all_gather(expert_key, 'wide', axis=0, tiled=True)  31.2 us
    all_gather x1, waiting for transfers between devices, shards(): lax.all_gather(expert_output, 'wide', axis=0, tiled=True)  29.5 us
    dot_general x1, matrix products, shards(): jnp.einsum('pd,kdc->pkc', normed, lax.all_gather(stacked, 'wide', axis=1,...  9.54 us
  transfers between devices with their start and end apart: 5, of which 5 were waited for; matrix products, arithmetic and copies ran while one was open for 7% of the time, Pallas kernels for 0%

commit v1 on v0

v1 whole, which is shorter than its diff:
```python
import functools

import jax
import jax.numpy as jnp
import numpy as np
from jax import lax
from jax.experimental import pallas as pl
from jax.experimental.pallas import tpu as pltpu
from jax.sharding import PartitionSpec as P

HEAD = 128
STEPS = 4
ROWS = 64

rope_base = 1000000.0
norm_eps = 1e-06


def rope_tables(rows):
    half = HEAD // 2
    inv = (np.float32(rope_base) ** (-np.arange(half, dtype=np.float32) * np.float32(2.0) / np.float32(HEAD))).astype(np.float32)
    angles = np.arange(rows, dtype=np.float32)[:, None] * inv[None, :]
    cosine, sine = np.cos(angles), np.sin(angles)
    return (
        np.concatenate([cosine, cosine], 1).astype(np.float32),
        np.concatenate([-sine, sine], 1).astype(np.float32),
    )


def time_embeddings(width):
    half = width // 2
    fraction = np.arange(half, dtype=np.float32) / np.float32(half - 1)
    period = np.float32(0.004) * np.float32(4.0 / 0.004) ** fraction
    rows = []
    for k in range(STEPS):
        angles = np.float32((1.0 - k / STEPS) * 2.0 * np.pi) / period
        rows.append(np.concatenate([np.sin(angles), np.cos(angles)]))
    return np.stack(rows).astype(np.float32)


def normalize(values, gain):
    mean_square = jnp.mean(values * values, axis=-1, keepdims=True)
    return values * lax.rsqrt(mean_square + norm_eps) * gain


def rotate(values, cosine, sine):
    return values * cosine + pltpu.roll(values, HEAD // 2, 1) * sine


def gather_kernel(
    nz, ny,
    key_ref, value_ref, query_ref, akey_ref, avalue_ref, out_ref, hidden_ref, gain_ref, cos_ref, sin_ref,
    k_out, v_out, e_out,
    buf, hid, normed, acc,
    own_sem, hid_sem, recv, zsend, ysend, xsend, csend, esem,
):
    kv_rows, kv = key_ref.shape
    e_rows, total = query_ref.shape[0], buf.shape[1]
    r1 = (total * 11 // 32 + 8) // 16 * 16
    r0 = total - 2 * r1
    g, w = lax.axis_index("groups"), lax.axis_index("wide")
    c, y, z = w % 2, (w // 2) % ny, w // (2 * ny)
    parity = g % 2

    def shard(zz, other_y, cc):
        yy = 1 - y if other_y else y
        return (zz * ny + yy) * 2 + cc

    def piece(k):
        if k == 0:
            return 0, r0, 0
        which = parity if k == 1 else 1 - parity
        return pl.multiple_of(r0 + which * r1, 16), r1, 1 + which

    core = {"wide": w + 1 - 2 * c}
    across = {"groups": g + 1 - 2 * parity}
    beside = {"wide": w + 2 - 4 * y} if ny > 1 else None

    def move(s, k, send, target):
        start, size, a = piece(k)
        part = buf.at[s, pl.ds(start, size), :]
        return pltpu.make_async_remote_copy(
            src_ref=part, dst_ref=part, send_sem=send, recv_sem=recv.at[s, a],
            device_id=target, device_id_type=pl.DeviceIdType.MESH,
        )

    def arrived(s, k):
        move(s, k, csend.at[0, 0], core).wait_recv()

    up, down = z + 1 < nz, z > 0

    def z_move(d, zz, k):
        return move(shard(zz, False, c), k, zsend.at[(d + 1) // 2, zz, k], {"wide": w + d * 2 * ny})

    def y_move(zz, k):
        return move(shard(zz, False, c), k, ysend.at[zz, k], beside)

    def x_move(zz, other_y):
        return move(shard(zz, other_y, c), 1, xsend.at[int(other_y), zz], across)

    def c_move(zz, other_y, k):
        return move(shard(zz, other_y, c), k, csend.at[int(other_y) * nz + zz, k], core)

    own = [
        (key_ref, buf.at[w, 0:kv_rows, 0:kv]),
        (value_ref, buf.at[w, 0:kv_rows, kv:2 * kv]),
        (query_ref, buf.at[w, kv_rows:kv_rows + e_rows, :]),
        (akey_ref, buf.at[w, kv_rows + e_rows:kv_rows + 2 * e_rows, 0:kv]),
        (avalue_ref, buf.at[w, kv_rows + e_rows:kv_rows + 2 * e_rows, kv:2 * kv]),
        (out_ref, buf.at[w, kv_rows + 2 * e_rows:total, :]),
    ]
    copies = [pltpu.make_async_copy(a, b, own_sem.at[i]) for i, (a, b) in enumerate(own)]
    for copy in copies:
        copy.start()
    hid_copy = pltpu.make_async_copy(hidden_ref.at[0], hid, hid_sem)
    hid_copy.start()

    barrier = pltpu.get_barrier_semaphore()

    def greet(target):
        pl.semaphore_signal(barrier, inc=1, device_id=target, device_id_type=pl.DeviceIdType.MESH)

    greet(core)
    greet(across)
    if ny > 1:
        greet(beside)

    @pl.when(up)
    def _():
        greet({"wide": w + 2 * ny})

    @pl.when(down)
    def _():
        greet({"wide": w - 2 * ny})

    pl.semaphore_wait(barrier, 2 + (ny > 1) + up.astype(jnp.int32) + down.astype(jnp.int32))
    for copy in copies:
        copy.wait()

    for k in (1, 0):
        @pl.when(up)
        def _():
            z_move(1, z, k).start()

        @pl.when(down)
        def _():
            z_move(-1, z, k).start()

        if ny > 1:
            y_move(z, k).start()
    for k in (1, 0, 2):
        c_move(z, False, k).start()

    hid_copy.wait()
    width = hid.shape[1]
    squares = jnp.zeros((hid.shape[0], HEAD), jnp.float32)

    def square(j, squares):
        part = hid[:, pl.ds(pl.multiple_of(j * HEAD, HEAD), HEAD)].astype(jnp.float32)
        return squares + part * part

    squares = lax.fori_loop(0, width // HEAD, square, squares)
    scale = lax.rsqrt(jnp.sum(squares, -1, keepdims=True) / width + norm_eps)
    wide_scale = jnp.broadcast_to(scale, (hid.shape[0], HEAD))
    per = kv_rows // HEAD

    def norm_part(j, carry):
        for i in range(per):
            at = pl.ds(pl.multiple_of((j * per + i) * HEAD, HEAD), HEAD)
            part = hid[:, at].astype(jnp.float32) * wide_scale * gain_ref[:, at]
            normed[j, :, i * HEAD:(i + 1) * HEAD] = part.astype(jnp.bfloat16)
        return carry

    lax.fori_loop(0, width // kv_rows, norm_part, 0)
    acc[...] = jnp.zeros_like(acc)

    def blocks(t, first, body):
        for d in (1, -1):
            zz = z - d * t
            ok = (zz >= 0) & (zz < nz) & (t >= first) & (t < nz)
            if d == -1:
                ok = ok & (t > 0)

            @pl.when(ok)
            def _():
                body(d, zz)

    def step(i, carry):
        for k in (1, 0):
            def line(d, zz, k=k):
                arrived(shard(zz, False, c), k)

                @pl.when((z + d >= 0) & (z + d < nz))
                def _():
                    z_move(d, zz, k).start()

                if ny > 1:
                    y_move(zz, k).start()
                if k == 1:
                    x_move(zz, False).start()
                c_move(zz, False, k).start()

            blocks(i, 1, line)
        if ny > 1:
            for k in (1, 0):
                def side(d, zz, k=k):
                    arrived(shard(zz, True, c), k)
                    if k == 1:
                        x_move(zz, True).start()
                    c_move(zz, True, k).start()

                blocks(i - 1, 0, side)
        for other_y in ((False, True) if ny > 1 else (False,)):
            def over(d, zz, other_y=other_y):
                arrived(shard(zz, other_y, c), 2)
                c_move(zz, other_y, 2).start()

            blocks(i - 2, 0 if other_y else 1, over)

        t = i - 3

        def use(q, carry):
            mine, yy, back = q % 2, (q // 2) % ny, q // (2 * ny)
            zz = z - t + back * 2 * t
            s = (zz * ny + (y + yy) % ny) * 2 + (c + mine) % 2

            @pl.when((zz >= 0) & (zz < nz) & (t >= 0) & ((back == 0) | (t > 0)))
            def _():
                @pl.when(mine == 1)
                def _():
                    for k in (1, 0, 2):
                        arrived(s, k)

                pltpu.make_async_copy(buf.at[s, kv_rows:total, :], e_out.at[s], esem.at[s]).start()
                acc[...] += jnp.dot(normed[s], buf[s, 0:kv_rows, :], preferred_element_type=jnp.float32)

            return carry

        return lax.fori_loop(0, 4 * ny, use, carry)

    lax.fori_loop(0, nz + 3, step, 0)

    rows = acc.shape[0]
    for h in range(kv // HEAD):
        at = slice(h * HEAD, (h + 1) * HEAD)
        k_out[:, at] = rotate(acc[:, at], cos_ref[...], sin_ref[...]).astype(jnp.bfloat16)
    v_out[...] = acc[:, kv:2 * kv].astype(jnp.bfloat16)

    def finish(t, carry):
        def line(d, zz):
            if ny > 1:
                for k in (1, 0):
                    y_move(zz, k).wait_send()

            @pl.when(t > 0)
            def _():
                x_move(zz, False).wait_send()

            for k in (1, 0, 2):
                c_move(zz, False, k).wait_send()
            if ny > 1:
                x_move(zz, True).wait_send()
                for k in (1, 0, 2):
                    c_move(zz, True, k).wait_send()

        def forward(d, zz):
            @pl.when((z + d >= 0) & (z + d < nz))
            def _():
                for k in (1, 0):
                    z_move(d, zz, k).wait_send()

        blocks(t, 0, line)
        blocks(t, 1, forward)
        return carry

    for k in (1, 0):
        @pl.when(up)
        def _():
            z_move(1, z, k).wait_send()

        @pl.when(down)
        def _():
            z_move(-1, z, k).wait_send()

    lax.fori_loop(0, nz, finish, 0)

    def drain(s, carry):
        pltpu.make_async_copy(buf.at[s, kv_rows:total, :], e_out.at[s], esem.at[s]).wait()
        return carry

    lax.fori_loop(0, buf.shape[0], drain, 0)


def steps_kernel(
    length_ref, noise_ref, input_ref, temb_ref, gain_ref, e_ref, final_ref, outw_ref, k_ref, v_ref, cos_ref, sin_ref,
    o_ref, state, keys, values, mixed,
):
    n, e3, width = e_ref.shape
    e_rows = e3 // 3
    span = noise_ref.shape[1]
    prefix, kv = k_ref.shape
    heads, kv_heads = width // HEAD, kv // HEAD
    ratio = heads // kv_heads
    length = length_ref[0]
    state[...] = jnp.zeros_like(state)
    state[0:span, :] = noise_ref[0]
    keys[0:prefix, :] = k_ref[...]
    values[0:prefix, :] = v_ref[...]
    cosine = cos_ref[pl.ds(length, ROWS), :]
    sine = sin_ref[pl.ds(length, ROWS), :]
    at = lax.broadcasted_iota(jnp.int32, (ratio * ROWS, prefix + ROWS), 1)
    valid = (at < length) | ((at >= prefix) & (at < prefix + span))

    def weight(i):
        return e_ref[:, i * e_rows:(i + 1) * e_rows, :].reshape(n * e_rows, width)

    def step(k, carry):
        hidden = jnp.dot(state[...], input_ref[...], precision=lax.Precision.HIGHEST, preferred_element_type=jnp.float32)
        hidden = hidden + temb_ref[pl.ds(k, 1), :]
        normed = normalize(hidden, gain_ref[...]).astype(jnp.bfloat16)
        raw = jnp.dot(normed, weight(1), preferred_element_type=jnp.float32)
        for h in range(kv_heads):
            cut = slice(h * HEAD, (h + 1) * HEAD)
            keys[prefix:, cut] = rotate(raw[:, cut], cosine, sine).astype(jnp.bfloat16)
        values[prefix:, :] = raw[:, kv:].astype(jnp.bfloat16)
        raw = jnp.dot(normed, weight(0), preferred_element_type=jnp.float32)
        for h in range(kv_heads):
            cut = slice(h * HEAD, (h + 1) * HEAD)
            queries = jnp.concatenate(
                [
                    (rotate(raw[:, j * HEAD:(j + 1) * HEAD], cosine, sine) * HEAD ** (-0.5)).astype(jnp.bfloat16)
                    for j in range(h * ratio, (h + 1) * ratio)
                ],
                0,
            )
            scores = lax.dot_general(queries, keys[:, cut], (((1,), (1,)), ((), ())), preferred_element_type=jnp.float32)
            scores = jnp.where(valid, scores, -1e30)
            weights = jnp.exp(scores - jnp.max(scores, -1, keepdims=True))
            probs = (weights / jnp.sum(weights, -1, keepdims=True)).astype(jnp.bfloat16)
            out = jnp.dot(probs, values[:, cut], preferred_element_type=jnp.float32).astype(jnp.bfloat16)
            for j in range(ratio):
                mixed[:, (h * ratio + j) * HEAD:(h * ratio + j + 1) * HEAD] = out[j * ROWS:(j + 1) * ROWS]
        hidden = hidden + jnp.dot(mixed[...], weight(2), preferred_element_type=jnp.float32)
        normed = normalize(hidden, final_ref[...]).astype(jnp.bfloat16)
        velocity = jnp.dot(normed, outw_ref[...], preferred_element_type=jnp.float32)
        state[...] = state[...] - velocity / STEPS
        return carry

    lax.fori_loop(0, STEPS, step, 0)
    o_ref[0] = state[0:span, :]


def shards(
    nz, ny,
    prefix_hidden, prefix_lengths, action_noise, prefix_gain, key_weight, value_weight, input_weight, expert_gain,
    expert_query, expert_key, expert_value, expert_output, final_gain, output_weight,
):
    n = nz * ny * 2
    prefix, width = prefix_hidden.shape[1:]
    kv_rows, kv = key_weight.shape
    e_rows, e_width = expert_query.shape
    total = kv_rows + 3 * e_rows
    span, dim = action_noise.shape[1:]
    cosine, sine = rope_tables(prefix + ROWS + 8)
    vmem, hbm = pl.BlockSpec(memory_space=pltpu.VMEM), pl.BlockSpec(memory_space=pl.ANY)
    bf16, f32 = jnp.bfloat16, jnp.float32
    dma = pltpu.SemaphoreType.DMA
    k_cache, v_cache, expert = pl.pallas_call(
        functools.partial(gather_kernel, nz, ny),
        out_shape=(
            jax.ShapeDtypeStruct((prefix, kv), bf16),
            jax.ShapeDtypeStruct((prefix, kv), bf16),
            jax.ShapeDtypeStruct((n, 3 * e_rows, e_width), bf16),
        ),
        in_specs=[hbm] * 7 + [vmem] * 3,
        out_specs=(vmem, vmem, hbm),
        scratch_shapes=[
            pltpu.VMEM((n, total, 2 * kv), bf16),
            pltpu.VMEM((prefix, width), bf16),
            pltpu.VMEM((n, prefix, kv_rows), bf16),
            pltpu.VMEM((prefix, 2 * kv), f32),
            dma((6,)),
            dma,
            dma((n, 3)),
            dma((2, nz, 2)),
            dma((nz, 2)),
            dma((2, nz)),
            dma((ny * nz, 3)),
            dma((n,)),
        ],
        compiler_params=pltpu.CompilerParams(collective_id=0, has_side_effects=True, vmem_limit_bytes=60 * 2 ** 20),
        name="gather",
    )(
        key_weight, value_weight, expert_query, expert_key, expert_value, expert_output,
        prefix_hidden, prefix_gain.reshape(1, -1), jnp.asarray(cosine[:prefix]), jnp.asarray(sine[:prefix]),
    )
    return pl.pallas_call(
        steps_kernel,
        out_shape=jax.ShapeDtypeStruct((1, span, dim), f32),
        in_specs=[pl.BlockSpec(memory_space=pltpu.SMEM)] + [vmem] * 11,
        out_specs=vmem,
        scratch_shapes=[
            pltpu.VMEM((ROWS, dim), f32),
            pltpu.VMEM((prefix + ROWS, kv), bf16),
            pltpu.VMEM((prefix + ROWS, kv), bf16),
            pltpu.VMEM((ROWS, e_width), bf16),
        ],
        name="steps",
    )(
        prefix_lengths, action_noise, input_weight, jnp.asarray(time_embeddings(e_width)), expert_gain.reshape(1, -1),
        expert, final_gain.reshape(1, -1), output_weight, k_cache, v_cache, jnp.asarray(cosine), jnp.asarray(sine),
    )


def solution(mesh):
    n = mesh.shape["wide"]
    column = mesh.devices[0] if mesh.axis_names[0] == "groups" else mesh.devices[:, 0]
    ny = len({d.coords[1] for d in column.flat}) if all(hasattr(d, "coords") for d in column.flat) else 1
    nz = n // (2 * ny)
    placed = (
        P(("groups", "wide"), None, None),
        P(("groups", "wide")),
        P(("groups", "wide"), None, None),
        P(),
        P("wide", None),
        P("wide", None),
        P(),
        P(),
        P("wide", None),
        P("wide", None),
        P("wide", None),
        P("wide", None),
        P(),
        P(),
    )
    return jax.shard_map(
        functools.partial(shards, nz, ny),
        mesh=mesh,
        in_specs=placed,
        out_specs=P(("groups", "wide"), None, None),
        check_vma=False,
    )
```

time: 369 us -> 122 us (0.33)
  waiting for transfers between devices: 266 us -> 0 us
  Pallas kernels: 0 us -> 117 us
  matrix products: 50.5 us -> 0 us
  other arithmetic: 16.4 us -> 0 us
  local copies, waits for them, and re-layouts: 20.1 us -> 4.54 us
  between operations: 15.1 us -> 0.66 us
    all_gather x5 -> x0, waiting for transfers between devices: 263 us -> none  [the longest x1 124 us: shards(): lax.all_gather(stacked, 'wide', axis=1, tiled=True)]
    pallas_call x0 -> x2, Pallas kernels: none -> 117 us  [the longest x1 99.8 us: shards(): pl.pallas_call(functools.partial(gather_kernel, nz, ny), out_shape=(jax.S...]
    dot_general x41 -> x0, matrix products: 50.5 us -> none  [the longest x1 9.54 us: shards(): jnp.einsum('pd,kdc->pkc', normed, lax.all_gather(stacked, 'wide', axis=1,...]
    reshape x12 -> x0, local copies, waits for them, and re-layouts: 7.68 us -> none  [the longest x4 4.41 us: attend(): own_values = action_values.reshape(span_rows, groups, HEAD)]
    reduce_sum x9 -> x0, other arithmetic: 6.5 us -> none  [the longest x4 3.15 us: attend(): jnp.sum(prefix_exp, -1, keepdims=True) + jnp.sum(own_exp, -1, keepdims=True)]
    convert_element_type x13 -> x0, local copies, waits for them, and re-layouts: 5.04 us -> none  [the longest x8 4.89 us: attend(): return attn_mixed.reshape(span_rows, -1).astype(jnp.bfloat16)]
    another operation x6 -> x0, other arithmetic: 4.08 us -> none  [the longest x1 2.26 us: shards(): stacked = jnp.stack([key_weight, value_weight], 0)]
  transfers between devices with their start and end apart: 5 -> 0, of which waited for: 5 -> 0; matrix products, arithmetic and copies ran while one was open for 7% -> 0% of each run, Pallas kernels for 0% -> 0%
where the time goes in v1:
time: 122 us
  Pallas kernels  117 us (96%)
  local copies, waits for them, and re-layouts  4.54 us (4%)
    pallas_call x1, Pallas kernels, shards(): pl.pallas_call(functools.partial(gather_kernel, nz, ny), out_shape=(jax.S...  99.8 us
    pallas_call x1, Pallas kernels, shards(): pl.pallas_call(steps_kernel, out_shape=jax.ShapeDtypeStruct((1, span, dim...  16.9 us
    unnamed x2, local copies, waits for them, and re-layouts  3.11 us

profile of v1, /device:TPU:0, one launch (start us, length us, event | category | flops | bytes accessed | tf_op | source)
XLA Modules:
  0.0 121.9 jit_solution(1111130240283144018)
XLA Ops:
  0.7 1.4 %copy.20.noise_ref = f32[1,50,32]{2,1,0:T(8,128)} copy(f32[1,50,32]{1,2,0:T(8,128)} %param.21) | data formatting | bytes 12800 | tf_op args[2]
  2.1 1.7 %copy.21.outw_ref = bf16[1024,32]{1,0:T(8,128)(2,1)} copy(bf16[1024,32]{0,1:T(8,128)(2,1)} %param.32) | data formatting | bytes 131072 | tf_op args[13]
  3.8 99.8 %gather.1 = (bf16[256,512]{1,0:T(8,128)(2,1)}, bf16[256,512]{1,0:T(8,128)(2,1)}, bf16[16,192,1024]{2,1,0:T(8,128)(2,1)}) custom-call(bf16[512,512]{1,0:T(8,128)(2,1)} %key_ref.1, bf16[512,512]{1,0:T(8,128)(2,1)} %value_ref.1, bf16[64,1024]{1,0:T(8,128)(2,1)} %query_ref.1, bf16[64,512]{1,0:T(8,128)(2,1)} %akey_ref.1, bf16[64,512]{1,0:T(8,128)(2,1)} %avalue_ref.1, ...), custom_call_target="tpu_custom_call" | custom-call | tf_op jit(solution)/shard_map/gather/pallas_call | solution.py:368
  103.5 16.9 %steps.1 = f32[1,50,32]{2,1,0:T(8,128)} custom-call(s32[1]{0:T(128)S(6)} %copy.23.length_ref, f32[1,50,32]{2,1,0:T(8,128)} %copy.20.noise_ref, f32[32,1024]{1,0:T(8,128)} %input_ref.1, f32[4,1024]{1,0:T(4,128)} %constant.12.clone.temb_ref, f32[1,1024]{1,0:T(1,128)} %bitcast.4, bf16[16,192,1024]{2,1,0:T(8,128)(2,1)} %get-tuple-element.8.e_ref, ...), custom_call_target="tpu_custom_call" | custom-call | tf_op jit(solution)/shard_map/steps/pallas_call | solution.py:397
  120.5 1.4 %copy.22 = f32[1,50,32]{1,2,0:T(8,128)} copy(f32[1,50,32]{2,1,0:T(8,128)} %steps.1) | data formatting | bytes 12800 | tf_op jit(solution)/shard_map/steps/pallas_call | solution.py:397

commit v2 on v1

--- a/solution.py
+++ b/solution.py
@@ -47,6 +47,12 @@
     return values * cosine + pltpu.roll(values, HEAD // 2, 1) * sine
 
 
+def share(total, ny):
+    if ny == 1:
+        return (total * 11 // 32 + 8) // 16 * 16, 0
+    return (total * 13 // 44 + 8) // 16 * 16, (total * 3 // 22 + 8) // 16 * 16
+
+
 def gather_kernel(
     nz, ny,
     key_ref, value_ref, query_ref, akey_ref, avalue_ref, out_ref, hidden_ref, gain_ref, cos_ref, sin_ref,
@@ -56,8 +62,8 @@
 ):
     kv_rows, kv = key_ref.shape
     e_rows, total = query_ref.shape[0], buf.shape[1]
-    r1 = (total * 11 // 32 + 8) // 16 * 16
-    r0 = total - 2 * r1
+    r1, rb = share(total, ny)
+    r0 = total - 2 * r1 - rb
     g, w = lax.axis_index("groups"), lax.axis_index("wide")
     c, y, z = w % 2, (w // 2) % ny, w // (2 * ny)
     parity = g % 2
@@ -69,8 +75,10 @@
     def piece(k):
         if k == 0:
             return 0, r0, 0
+        if k == 3:
+            return r0, rb, 3
         which = parity if k == 1 else 1 - parity
-        return pl.multiple_of(r0 + which * r1, 16), r1, 1 + which
+        return pl.multiple_of(r0 + rb + which * r1, 16), r1, 1 + which
 
     core = {"wide": w + 1 - 2 * c}
     across = {"groups": g + 1 - 2 * parity}
@@ -88,12 +96,16 @@
         move(s, k, csend.at[0, 0], core).wait_recv()
 
     up, down = z + 1 < nz, z > 0
+    every = (1, 0, 2, 3) if ny > 1 else (1, 0, 2)
 
     def z_move(d, zz, k):
         return move(shard(zz, False, c), k, zsend.at[(d + 1) // 2, zz, k], {"wide": w + d * 2 * ny})
 
+    def b_move(d, zz, other_y):
+        return move(shard(zz, other_y, c), 3, zsend.at[(d + 1) // 2, zz, 2 + other_y], {"wide": w + d * 2 * ny})
+
     def y_move(zz, k):
-        return move(shard(zz, False, c), k, ysend.at[zz, k], beside)
+        return move(shard(zz, False, c), k, ysend.at[zz, min(k, 2)], beside)
 
     def x_move(zz, other_y):
         return move(shard(zz, other_y, c), 1, xsend.at[int(other_y), zz], across)
@@ -148,7 +160,9 @@
 
         if ny > 1:
             y_move(z, k).start()
-    for k in (1, 0, 2):
+    if ny > 1:
+        y_move(z, 3).start()
+    for k in every:
         c_move(z, False, k).start()
 
     hid_copy.wait()
@@ -185,6 +199,16 @@
             def _():
                 body(d, zz)
 
+    def slot(j, first, body):
+        paired = jnp.minimum(z, nz - 1 - z)
+        t = jnp.where(j <= 2 * paired, (j + 1) // 2, j - paired)
+        below = jnp.where(j <= 2 * paired, j % 2, (z > nz - 1 - z).astype(jnp.int32))
+        zz = z + t - 2 * below * t
+
+        @pl.when((j >= first) & (j < nz))
+        def _():
+            body(zz)
+
     def step(i, carry):
         for k in (1, 0):
             def line(d, zz, k=k):
@@ -194,49 +218,84 @@
                 def _():
                     z_move(d, zz, k).start()
 
-                if ny > 1:
-                    y_move(zz, k).start()
                 if k == 1:
                     x_move(zz, False).start()
+                if ny > 1:
+                    if d == 1:
+                        y_move(zz, k).start()
+                    else:
+                        @pl.when((z - i >= 0) == (k == 0))
+                        def _():
+                            y_move(zz, 1).start()
+
+                        if k == 0:
+                            y_move(zz, 0).start()
                 c_move(zz, False, k).start()
 
             blocks(i, 1, line)
+        def side(k):
+            def body(zz):
+                arrived(shard(zz, True, c), k)
+                if k == 1:
+                    x_move(zz, True).start()
+                c_move(zz, True, k).start()
+
+            slot(i - 1, 0, body)
+
+        def both(d, zz):
+            for other_y in (False, True):
+                arrived(shard(zz, other_y, c), 3)
+
+                @pl.when((z + d >= 0) & (z + d < nz))
+                def _():
+                    b_move(d, zz, other_y).start()
+
+                c_move(zz, other_y, 3).start()
+
         if ny > 1:
-            for k in (1, 0):
-                def side(d, zz, k=k):
-                    arrived(shard(zz, True, c), k)
-                    if k == 1:
-                        x_move(zz, True).start()
-                    c_move(zz, True, k).start()
-
-                blocks(i - 1, 0, side)
+            side(1)
+
+            @pl.when(i == 2)
+            def _():
+                arrived(shard(z, True, c), 3)
+                for other_y in (False, True):
+                    @pl.when(up)
+                    def _():
+                        b_move(1, z, other_y).start()
+
+                    @pl.when(down)
+                    def _():
+                        b_move(-1, z, other_y).start()
+
+                c_move(z, True, 3).start()
+
+            blocks(i - 2, 1, both)
+            side(0)
         for other_y in ((False, True) if ny > 1 else (False,)):
-            def over(d, zz, other_y=other_y):
+            def over(zz, other_y=other_y):
                 arrived(shard(zz, other_y, c), 2)
                 c_move(zz, other_y, 2).start()
 
-            blocks(i - 2, 0 if other_y else 1, over)
-
-        t = i - 3
-
-        def use(q, carry):
-            mine, yy, back = q % 2, (q // 2) % ny, q // (2 * ny)
-            zz = z - t + back * 2 * t
-            s = (zz * ny + (y + yy) % ny) * 2 + (c + mine) % 2
-
-            @pl.when((zz >= 0) & (zz < nz) & (t >= 0) & ((back == 0) | (t > 0)))
-            def _():
+            slot(i - 2, 0 if other_y else 1, over)
+
+        def pair(zz):
+            def use(q, carry):
+                mine, yy = q % 2, q // 2
+                s = (zz * ny + (y + yy) % ny) * 2 + (c + mine) % 2
+
                 @pl.when(mine == 1)
                 def _():
-                    for k in (1, 0, 2):
+                    for k in every:
                         arrived(s, k)
 
                 pltpu.make_async_copy(buf.at[s, kv_rows:total, :], e_out.at[s], esem.at[s]).start()
                 acc[...] += jnp.dot(normed[s], buf[s, 0:kv_rows, :], preferred_element_type=jnp.float32)
-
-            return carry
-
-        return lax.fori_loop(0, 4 * ny, use, carry)
+                return carry
+
+            lax.fori_loop(0, 2 * ny, use, 0)
+
+        slot(i - 3, 0, pair)
+        return carry
 
     lax.fori_loop(0, nz + 3, step, 0)
 
@@ -256,11 +315,11 @@
             def _():
                 x_move(zz, False).wait_send()
 
-            for k in (1, 0, 2):
+            for k in every:
                 c_move(zz, False, k).wait_send()
             if ny > 1:
                 x_move(zz, True).wait_send()
-                for k in (1, 0, 2):
+                for k in every:
                     c_move(zz, True, k).wait_send()
 
         def forward(d, zz):
@@ -268,19 +327,32 @@
             def _():
                 for k in (1, 0):
                     z_move(d, zz, k).wait_send()
+                if ny > 1:
+                    for other_y in (False, True):
+                        b_move(d, zz, other_y).wait_send()
 
         blocks(t, 0, line)
         blocks(t, 1, forward)
         return carry
 
-    for k in (1, 0):
-        @pl.when(up)
-        def _():
+    @pl.when(up)
+    def _():
+        for k in (1, 0):
             z_move(1, z, k).wait_send()
-
-        @pl.when(down)
-        def _():
+        if ny > 1:
+            for other_y in (False, True):
+                b_move(1, z, other_y).wait_send()
+
+    @pl.when(down)
+    def _():
+        for k in (1, 0):
             z_move(-1, z, k).wait_send()
+        if ny > 1:
+            for other_y in (False, True):
+                b_move(-1, z, other_y).wait_send()
+
+    if ny > 1:
+        y_move(z, 3).wait_send()
 
     lax.fori_loop(0, nz, finish, 0)
 
@@ -297,13 +369,13 @@
 ):
     n, e3, width = e_ref.shape
     e_rows = e3 // 3
-    span = noise_ref.shape[1]
+    span = noise_ref.shape[2]
     prefix, kv = k_ref.shape
     heads, kv_heads = width // HEAD, kv // HEAD
     ratio = heads // kv_heads
     length = length_ref[0]
     state[...] = jnp.zeros_like(state)
-    state[0:span, :] = noise_ref[0]
+    state[:, 0:span] = noise_ref[0]
     keys[0:prefix, :] = k_ref[...]
     values[0:prefix, :] = v_ref[...]
     cosine = cos_ref[pl.ds(length, ROWS), :]
@@ -315,7 +387,10 @@
         return e_ref[:, i * e_rows:(i + 1) * e_rows, :].reshape(n * e_rows, width)
 
     def step(k, carry):
-        hidden = jnp.dot(state[...], input_ref[...], precision=lax.Precision.HIGHEST, preferred_element_type=jnp.float32)
+        hidden = lax.dot_general(
+            state[...], input_ref[...], (((0,), (0,)), ((), ())),
+            precision=lax.Precision.HIGHEST, preferred_element_type=jnp.float32,
+        )
         hidden = hidden + temb_ref[pl.ds(k, 1), :]
         normed = normalize(hidden, gain_ref[...]).astype(jnp.bfloat16)
         raw = jnp.dot(normed, weight(1), preferred_element_type=jnp.float32)
@@ -342,12 +417,12 @@
                 mixed[:, (h * ratio + j) * HEAD:(h * ratio + j + 1) * HEAD] = out[j * ROWS:(j + 1) * ROWS]
         hidden = hidden + jnp.dot(mixed[...], weight(2), preferred_element_type=jnp.float32)
         normed = normalize(hidden, final_ref[...]).astype(jnp.bfloat16)
-        velocity = jnp.dot(normed, outw_ref[...], preferred_element_type=jnp.float32)
+        velocity = lax.dot_general(outw_ref[...], normed, (((1,), (1,)), ((), ())), preferred_element_type=jnp.float32)
         state[...] = state[...] - velocity / STEPS
         return carry
 
     lax.fori_loop(0, STEPS, step, 0)
-    o_ref[0] = state[0:span, :]
+    o_ref[0] = state[:, 0:span]
 
 
 def shards(
@@ -381,11 +456,11 @@
             pltpu.VMEM((prefix, 2 * kv), f32),
             dma((6,)),
             dma,
-            dma((n, 3)),
-            dma((2, nz, 2)),
-            dma((nz, 2)),
+            dma((n, 4)),
+            dma((2, nz, 4)),
+            dma((nz, 3)),
             dma((2, nz)),
-            dma((ny * nz, 3)),
+            dma((ny * nz, 4)),
             dma((n,)),
         ],
         compiler_params=pltpu.CompilerParams(collective_id=0, has_side_effects=True, vmem_limit_bytes=60 * 2 ** 20),
@@ -394,22 +469,23 @@
         key_weight, value_weight, expert_query, expert_key, expert_value, expert_output,
         prefix_hidden, prefix_gain.reshape(1, -1), jnp.asarray(cosine[:prefix]), jnp.asarray(sine[:prefix]),
     )
-    return pl.pallas_call(
+    actions = pl.pallas_call(
         steps_kernel,
-        out_shape=jax.ShapeDtypeStruct((1, span, dim), f32),
+        out_shape=jax.ShapeDtypeStruct((1, dim, span), f32),
         in_specs=[pl.BlockSpec(memory_space=pltpu.SMEM)] + [vmem] * 11,
         out_specs=vmem,
         scratch_shapes=[
-            pltpu.VMEM((ROWS, dim), f32),
+            pltpu.VMEM((dim, ROWS), f32),
             pltpu.VMEM((prefix + ROWS, kv), bf16),
             pltpu.VMEM((prefix + ROWS, kv), bf16),
             pltpu.VMEM((ROWS, e_width), bf16),
         ],
         name="steps",
     )(
-        prefix_lengths, action_noise, input_weight, jnp.asarray(time_embeddings(e_width)), expert_gain.reshape(1, -1),
-        expert, final_gain.reshape(1, -1), output_weight, k_cache, v_cache, jnp.asarray(cosine), jnp.asarray(sine),
+        prefix_lengths, action_noise.transpose(0, 2, 1), input_weight, jnp.asarray(time_embeddings(e_width)), expert_gain.reshape(1, -1),
+        expert, final_gain.reshape(1, -1), output_weight.T, k_cache, v_cache, jnp.asarray(cosine), jnp.asarray(sine),
     )
+    return actions.transpose(0, 2, 1)
 
 
 def solution(mesh):

time: 122 us -> 110 us (0.902)
  Pallas kernels: 117 us -> 109 us
  local copies, waits for them, and re-layouts: 4.54 us -> 0 us
    pallas_call x1, Pallas kernels: 99.8 us -> 92.2 us  [shards(): pl.pallas_call(functools.partial(gather_kernel, nz, ny), out_shape=(jax.S...]
    unnamed x2 -> x0, local copies, waits for them, and re-layouts: 3.11 us -> none
    pallas_call x1 -> x0, local copies, waits for them, and re-layouts: 1.43 us -> none  [shards(): pl.pallas_call(steps_kernel, out_shape=jax.ShapeDtypeStruct((1, span, dim...]
where the time goes in v2:
time: 110 us
  Pallas kernels  109 us (99%)
    pallas_call x1, Pallas kernels, shards(): pl.pallas_call(functools.partial(gather_kernel, nz, ny), out_shape=(jax.S...  92.2 us
    pallas_call x1, Pallas kernels, shards(): pl.pallas_call(steps_kernel, out_shape=jax.ShapeDtypeStruct((1, dim, span...  17.2 us

profile of v2, /device:TPU:0, one launch (start us, length us, event | category | flops | bytes accessed | tf_op | source)
XLA Modules:
  0.0 110.0 jit_solution(13217184604912149723)
XLA Ops:
  0.7 92.2 %gather.1 = (bf16[256,512]{1,0:T(8,128)(2,1)}, bf16[256,512]{1,0:T(8,128)(2,1)}, bf16[16,192,1024]{2,1,0:T(8,128)(2,1)}) custom-call(bf16[512,512]{1,0:T(8,128)(2,1)} %key_ref.1, bf16[512,512]{1,0:T(8,128)(2,1)} %value_ref.1, bf16[64,1024]{1,0:T(8,128)(2,1)} %query_ref.1, bf16[64,512]{1,0:T(8,128)(2,1)} %akey_ref.1, bf16[64,512]{1,0:T(8,128)(2,1)} %avalue_ref.1, ...), custom_call_target="tpu_custom_call" | custom-call | tf_op jit(solution)/shard_map/gather/pallas_call | solution.py:443
  92.8 17.2 %steps.1 = f32[1,32,50]{2,1,0:T(8,128)} custom-call(s32[1]{0:T(128)S(6)} %copy.20.length_ref, f32[1,32,50]{2,1,0:T(8,128)} %bitcast.8, f32[32,1024]{1,0:T(8,128)} %input_ref.1, f32[4,1024]{1,0:T(4,128)} %constant.12.clone.temb_ref, f32[1,1024]{1,0:T(1,128)} %bitcast.9, bf16[16,192,1024]{2,1,0:T(8,128)(2,1)} %get-tuple-element.8.e_ref, f32[1,1024]{1,0:T(1,128)} %bitcast.10, ...), custom_call_target="tpu_custom_call" | custom-call | tf_op jit(solution)/shard_map/steps/pallas_call | solution.py:472

commit v3 on v2

--- a/solution.py
+++ b/solution.py
@@ -209,6 +209,24 @@
         def _():
             body(zz)
 
+    def consume(zz, mine):
+        def use(yy, carry):
+            s = (zz * ny + (y + yy) % ny) * 2 + (c + mine) % 2
+            if mine:
+                for k in every:
+                    arrived(s, k)
+            pltpu.make_async_copy(buf.at[s, kv_rows:total, :], e_out.at[s], esem.at[s]).start()
+            acc[...] += jnp.dot(normed[s], buf[s, 0:kv_rows, :], preferred_element_type=jnp.float32)
+            return carry
+
+        lax.fori_loop(0, ny, use, 0)
+
+    def ours(zz):
+        consume(zz, 0)
+
+    def theirs(zz):
+        consume(zz, 1)
+
     def step(i, carry):
         for k in (1, 0):
             def line(d, zz, k=k):
@@ -254,7 +272,8 @@
 
         if ny > 1:
             side(1)
-
+        pl.when(i == nz + 1)(lambda: slot(i - 3, 0, theirs))
+        if ny > 1:
             @pl.when(i == 2)
             def _():
                 arrived(shard(z, True, c), 3)
@@ -278,23 +297,8 @@
 
             slot(i - 2, 0 if other_y else 1, over)
 
-        def pair(zz):
-            def use(q, carry):
-                mine, yy = q % 2, q // 2
-                s = (zz * ny + (y + yy) % ny) * 2 + (c + mine) % 2
-
-                @pl.when(mine == 1)
-                def _():
-                    for k in every:
-                        arrived(s, k)
-
-                pltpu.make_async_copy(buf.at[s, kv_rows:total, :], e_out.at[s], esem.at[s]).start()
-                acc[...] += jnp.dot(normed[s], buf[s, 0:kv_rows, :], preferred_element_type=jnp.float32)
-                return carry
-
-            lax.fori_loop(0, 2 * ny, use, 0)
-
-        slot(i - 3, 0, pair)
+        pl.when(i != nz + 1)(lambda: slot(i - 3, 0, theirs))
+        slot(i - 2, 0, ours)
         return carry
 
     lax.fori_loop(0, nz + 3, step, 0)

time: 110 us -> 109 us (level)
    pallas_call x1, Pallas kernels: 92.2 us -> 91 us  [shards(): pl.pallas_call(functools.partial(gather_kernel, nz, ny), out_shape=(jax.S...]
where the time goes in v3:
time: 109 us
  Pallas kernels  108 us (99%)
    pallas_call x1, Pallas kernels, shards(): pl.pallas_call(functools.partial(gather_kernel, nz, ny), out_shape=(jax.S...  91 us
    pallas_call x1, Pallas kernels, shards(): pl.pallas_call(steps_kernel, out_shape=jax.ShapeDtypeStruct((1, dim, span...  17.2 us

profile of v3, /device:TPU:0, one launch (start us, length us, event | category | flops | bytes accessed | tf_op | source)
XLA Modules:
  0.0 108.8 jit_solution(16434143873243026446)
XLA Ops:
  0.7 91.0 %gather.1 = (bf16[256,512]{1,0:T(8,128)(2,1)}, bf16[256,512]{1,0:T(8,128)(2,1)}, bf16[16,192,1024]{2,1,0:T(8,128)(2,1)}) custom-call(bf16[512,512]{1,0:T(8,128)(2,1)} %key_ref.1, bf16[512,512]{1,0:T(8,128)(2,1)} %value_ref.1, bf16[64,1024]{1,0:T(8,128)(2,1)} %query_ref.1, bf16[64,512]{1,0:T(8,128)(2,1)} %akey_ref.1, bf16[64,512]{1,0:T(8,128)(2,1)} %avalue_ref.1, ...), custom_call_target="tpu_custom_call" | custom-call | tf_op jit(solution)/shard_map/gather/pallas_call | solution.py:447
  91.6 17.2 %steps.1 = f32[1,32,50]{2,1,0:T(8,128)} custom-call(s32[1]{0:T(128)S(6)} %copy.20.length_ref, f32[1,32,50]{2,1,0:T(8,128)} %bitcast.8, f32[32,1024]{1,0:T(8,128)} %input_ref.1, f32[4,1024]{1,0:T(4,128)} %constant.12.clone.temb_ref, f32[1,1024]{1,0:T(1,128)} %bitcast.9, bf16[16,192,1024]{2,1,0:T(8,128)(2,1)} %get-tuple-element.8.e_ref, f32[1,1024]{1,0:T(1,128)} %bitcast.10, ...), custom_call_target="tpu_custom_call" | custom-call | tf_op jit(solution)/shard_map/steps/pallas_call | solution.py:476
